TPU v7x, 32 devices: a whole 2x2x4 slice. The times are simulated.
32 devices in a mesh: tile: 8 (over z, y), depth: 4 (over x, core).
Axes of the slice: x: 2, y: 2, z: 4, core: 2. Of those that a mesh axis runs over, the one named last changes fastest.
Arguments:
- owned_blocks: bfloat16 [4, 512, 32768], P('depth', 'tile'), may hold values from -6 to 6
- slot_counts: int32 [4, 8], P('depth'), may hold values from 1 to 64, 256 in all within a row
- brick_order: int32 [4, 8], P('depth'), may hold values from 0 to 7, each once within a row
- view_flip: int32 [8], replicated, may hold values from 0 to 1
- tf_centers: float32 [8], replicated, may hold values from -2.5 to 2.5
- tf_amps: float32 [4, 8], replicated, may hold values from -6 to 6
Outputs:
- image: float32 [4, 128, 1024], P(None, 'depth', 'tile')
Inputs may be any that keep to these rules, and one draw needn't show every extreme that they name: `slot_counts`: every row sums to 256, and some entry of every row equals 64. `brick_order`: every row holds each of 0 to 7 once.
All inputs are finite; a program needn't handle non-finite values.
Results may differ from a plain program's by a relative error of at most 0.0003.
Values may be sent and summed in bfloat16 or wider, within the bound.
No kernel may reach another device: no remote copies, remote signals or barrier semaphores. Data moves between devices by JAX's collectives and lax.ppermute only.
A program may use at most 64 MiB of HBM per device.

v0:
```python
import functools
import math

import jax
import jax.numpy as jnp
from jax import lax
from jax.experimental import pallas as pl
from jax.experimental.pallas import tpu as pltpu
from jax.sharding import PartitionSpec as P

BLOCK = 32
BX = 4
BY = 4
DB = 2
KNOTS = 8
PIXELS = BLOCK * BLOCK
LANES = 128
TILES = PIXELS // LANES
BUMP_SCALE = 4.0
LOG2E = math.log2(math.e)
ROOT = math.sqrt(BUMP_SCALE * LOG2E)
CODE_TOP = 65535.0
CODE_MID = 32767.5
GRANT = 12 << 20
SPAN = 512
GROUPS = PIXELS // SPAN
STACK = 8 * GROUPS
PACK = 16 // 8


def exclusive_start(counts_ref, index, tile_count):
    start = jnp.int32(0)
    for i in range(tile_count):
        start = start + jnp.where(i < index, counts_ref[i], 0)
    return start


def position_of(order_ref, tile, tile_count):
    position = jnp.int32(0)
    for i in range(tile_count):
        position = position + jnp.where(order_ref[i] == tile, i, 0)
    return position


def encode(image):
    root = jnp.exp2(jnp.log(jnp.maximum(image, 0.0)) * (0.25 * LOG2E))
    code = jnp.round(jnp.minimum(root, 1.0) * CODE_TOP - CODE_MID)
    return code.astype(jnp.int32).astype(jnp.int16)


def decode(code):
    root = (code.astype(jnp.int32).astype(jnp.float32) + CODE_MID) * (1.0 / CODE_TOP)
    square = root * root
    return square * square


def march_kernel(step_size, tile_count, relative, *refs):
    counts_ref, order_ref, flip_ref, me_ref, center_ref, amp_ref, cells_ref = refs[:7]
    outs = refs[7:7 + relative]
    coef_ref, mix_ref, stage_ref, slot_ref = refs[7 + relative:]
    step = pl.program_id(0)
    me = me_ref[0]
    start = exclusive_start(counts_ref, me, tile_count)
    live = counts_ref[me]

    @pl.when(step == 0)
    def _():
        for r in range(relative):
            tile = lax.rem(me + r, tile_count)
            slot_ref[r] = lax.rem(
                position_of(order_ref, tile, tile_count) - start + tile_count * 64, tile_count
            )
        w = center_ref[...] * ROOT
        folded = amp_ref[...] * jnp.exp2(-w * w)
        channel = lax.broadcasted_iota(jnp.int32, (4, 1), 0)
        folded = folded * jnp.where(channel == 3, LOG2E, 0.5)
        for k in range(KNOTS):
            coef_ref[k] = jnp.broadcast_to(2.0 * w[:, k:k + 1], (8, LANES))
        knot = lax.broadcasted_iota(jnp.int32, (4, KNOTS * STACK), 1) // STACK
        spread = jnp.zeros((4, KNOTS * STACK), jnp.float32)
        for k in range(KNOTS):
            spread = jnp.where(knot == k, folded[:, k:k + 1], spread)
        coarse = spread.astype(jnp.bfloat16)
        fine = (spread - coarse.astype(jnp.float32)).astype(jnp.bfloat16)
        own = lax.broadcasted_iota(jnp.int32, (STACK, KNOTS * STACK), 0) == lax.rem(
            lax.broadcasted_iota(jnp.int32, (STACK, KNOTS * STACK), 1), STACK
        )
        width = KNOTS * STACK
        for part, amps in enumerate((coarse, fine)):
            amps = amps.astype(jnp.float32)
            for c in range(4):
                first = (part * 4 + c) * STACK
                line = jnp.where(own, amps[c:c + 1], 0.0).astype(jnp.bfloat16)
                mix_ref[first:first + STACK, :width] = line
                mix_ref[first:first + STACK, width:] = line

    @pl.when(step * tile_count < live)
    def _():
        row = lax.broadcasted_iota(jnp.int32, (8, SPAN), 0)
        for half in range(tile_count // 8):
            flip = jnp.zeros((8, SPAN), jnp.int32)
            for s in range(8):
                tile = order_ref[lax.rem(start + half * 8 + s, tile_count)]
                flip = jnp.where(row == s, flip_ref[tile], flip)
            down = flip == 1
            signed_step = jnp.where(down, step_size, -step_size)

            def depth(z, state, half=half, signed_step=signed_step):
                values = []
                for j in range(GROUPS):
                    lane = pl.multiple_of(z * PIXELS + j * SPAN, LANES)
                    raw = cells_ref[half * 8:half * 8 + 8, pl.ds(lane, SPAN)]
                    values.append(raw.astype(jnp.float32) * ROOT)
                bumps = []
                for k in range(KNOTS):
                    center = jnp.concatenate([coef_ref[k]] * (SPAN // LANES), axis=1)
                    bumps += [jnp.exp2(v * (center - v)) for v in values]
                high, low = [], []
                for n in range(0, len(bumps), PACK):
                    bump = jnp.concatenate(bumps[n:n + PACK], axis=0)
                    coarse = bump.astype(jnp.bfloat16)
                    high.append(coarse)
                    low.append((bump - coarse.astype(jnp.float32)).astype(jnp.bfloat16))
                stacked = jnp.concatenate(high + low, axis=0)
                both = jnp.dot(mix_ref[...], stacked, preferred_element_type=jnp.float32)
                fields = both[:4 * STACK] + both[4 * STACK:]
                after = []
                for j in range(GROUPS):
                    red, green, blue, dense = (
                        fields[c * STACK + j * 8:c * STACK + j * 8 + 8] for c in range(4)
                    )
                    total, seen, reds, greens, blues = state[j]
                    total = total + lax.log2(1.0 + jnp.exp2(dense))
                    now = jnp.exp2(signed_step * total)
                    weight = now - seen
                    after.append((
                        total,
                        now,
                        reds + weight * jnp.tanh(red),
                        greens + weight * jnp.tanh(green),
                        blues + weight * jnp.tanh(blue),
                    ))
                return tuple(after)

            zero = jnp.zeros((8, SPAN), jnp.float32)
            first = tuple((zero, zero + 1.0, zero, zero, zero) for j in range(GROUPS))
            last = lax.fori_loop(0, BLOCK, depth, first, unroll=True)
            for j in range(GROUPS):
                total, seen, reds, greens, blues = last[j]
                passed = jnp.exp2(total * -step_size)
                factor = jnp.where(down, 0.5 * passed, -0.5)
                spread = seen - 1.0
                planes = [factor * (spread + color) for color in (reds, greens, blues)]
                planes.append(1.0 - passed)
                for c in range(4):
                    for i in range(SPAN // LANES):
                        rows = pl.ds(j * (SPAN // LANES) + i, 8, stride=TILES)
                        stage_ref[half, c, rows, :] = planes[c][:, i * LANES:(i + 1) * LANES]
        for r in range(relative):
            slot = slot_ref[r]
            rows = pl.ds(pl.multiple_of(lax.rem(slot, 8) * TILES, TILES), TILES)
            for c in range(4):
                outs[r][0, c] = encode(stage_ref[slot // 8, c, rows, :])


def pinned(array):
    return pltpu.with_memory_space_constraint(array, pltpu.HBM)


def march(counts, order, flip, me, centers, amps, cells, step_size):
    tile_count = counts.shape[0]
    slots = cells.shape[0]
    capacity = slots // tile_count
    scalar = pl.BlockSpec(memory_space=pltpu.SMEM)
    whole = lambda shape: pl.BlockSpec(shape, lambda m: (0,) * len(shape))
    block = pl.BlockSpec((1, 4, TILES, LANES), lambda m: (m, 0, 0, 0))
    return pl.pallas_call(
        functools.partial(march_kernel, step_size, tile_count, tile_count),
        grid=(capacity,),
        in_specs=[scalar] * 4 + [
            whole((1, KNOTS)),
            whole((4, KNOTS)),
            pl.BlockSpec((tile_count, cells.shape[1]), lambda m: (m, 0)),
        ],
        out_specs=[block] * tile_count,
        out_shape=[jax.ShapeDtypeStruct((capacity, 4, TILES, LANES), jnp.int16)] * tile_count,
        scratch_shapes=[
            pltpu.VMEM((KNOTS, 8, LANES), jnp.float32),
            pltpu.VMEM((8 * STACK, 2 * KNOTS * STACK), jnp.bfloat16),
            pltpu.VMEM((tile_count // 8, 4, 8 * TILES, LANES), jnp.float32),
            pltpu.SMEM((tile_count,), jnp.int32),
        ],
        compiler_params=pltpu.CompilerParams(vmem_limit_bytes=GRANT),
        name="march",
    )(*(pinned(x) for x in (counts, order, flip, me, centers.reshape(1, KNOTS), amps, cells)))


def split_rows(image, kept_ref, given_ref, low, row_share):
    for n in range(kept_ref.shape[1] // row_share):
        mine = pl.multiple_of((2 * n + low) * row_share, row_share)
        theirs = pl.multiple_of((2 * n + 1 - low) * row_share, row_share)
        for c in range(4):
            kept_ref[c, n * row_share:(n + 1) * row_share] = image[c, pl.ds(mine, row_share)]
            given_ref[c, n * row_share:(n + 1) * row_share] = encode(image[c, pl.ds(theirs, row_share)])


def place_images(counts_ref, order_ref, me, brick_ref, arrived, tile_count):
    position = position_of(order_ref, me, tile_count)
    starts = [jnp.int32(0)]
    for i in range(tile_count):
        starts.append(starts[-1] + counts_ref[i])
    for r, images_ref in arrived:
        owner = lax.rem(me - r + tile_count, tile_count)
        start = jnp.int32(0)
        for i in range(tile_count):
            start = jnp.where(owner == i, starts[i], start)
        offset = lax.rem(position - start + tile_count * 64, tile_count)
        level = (start + offset - position) // tile_count
        held = (counts_ref[owner] - offset + tile_count - 1) // tile_count

        def place(m, carry, images_ref=images_ref, level=level):
            brick_ref[level + m] = decode(images_ref[m])
            return carry

        lax.fori_loop(0, held, place, 0)


def place_kernel(tile_count, *refs):
    counts_ref, order_ref, me_ref = refs[:3]
    arrived = [(r, ref) for r, ref in enumerate(refs[3:-1])]
    place_images(counts_ref, order_ref, me_ref[0], refs[-1], arrived, tile_count)


def place_early(counts, order, me, arrived):
    tile_count = counts.shape[0]
    scalar = pl.BlockSpec(memory_space=pltpu.SMEM)
    vmem = pl.BlockSpec(memory_space=pltpu.VMEM)
    brick = (DB * BY * BX, 4, TILES, LANES)
    return pl.pallas_call(
        functools.partial(place_kernel, tile_count),
        in_specs=[scalar] * 3 + [vmem] * len(arrived),
        out_specs=vmem,
        out_shape=jax.ShapeDtypeStruct(brick, jnp.float32),
        compiler_params=pltpu.CompilerParams(vmem_limit_bytes=GRANT),
        cost_estimate=pl.CostEstimate(flops=1 << 20, bytes_accessed=1 << 20, transcendentals=0),
        name="place",
    )(counts, order, me, *arrived)


def gather_kernel(tile_count, row_share, last_bit, *refs):
    counts_ref, order_ref, flip_ref, me_ref, layer_ref, early_ref = refs[:6]
    kept_ref, given_ref, front_ref, brick_ref, image_ref = refs[-5:]
    late = refs[6:-5]
    me = me_ref[0]
    brick_ref[...] = early_ref[...]
    arrived = [(tile_count - len(late) + n, ref) for n, ref in enumerate(late)]
    place_images(counts_ref, order_ref, me, brick_ref, arrived, tile_count)
    flip = flip_ref[me] == 1
    lane = lax.broadcasted_iota(jnp.int32, (TILES, LANES), 1) // BLOCK
    per_row = LANES // BLOCK
    for by in range(BY):
        images = []
        for bx in range(BX):
            layers = [(bz * BY + by) * BX + bx for bz in range(DB)]
            parts = None
            for n in range(DB):
                index = jnp.where(flip, layers[n], layers[DB - 1 - n])
                new = [brick_ref[index, c] for c in range(4)]
                if parts is None:
                    parts = new
                else:
                    uncovered = 1.0 - new[3]
                    parts = [new[c] + uncovered * parts[c] for c in range(4)]
            images.append(parts)
        for c in range(4):
            for s in range(per_row):
                line = None
                for bx in range(BX):
                    turn = (bx - s) * BLOCK % LANES
                    moved = images[bx][c]
                    if turn:
                        moved = pltpu.roll(moved, turn, 1)
                    line = moved if line is None else jnp.where(lane == bx, moved, line)
                image_ref[c, pl.ds(by * BLOCK + s, TILES, stride=per_row), :] = line
    split_rows(image_ref, kept_ref, given_ref, layer_ref[0] & 1, row_share)
    front = (layer_ref[0] >> last_bit & 1) == flip_ref[me]
    front_ref[...] = jnp.broadcast_to(jnp.where(front, 1.0, 0.0), (8, LANES))


def gather(counts, order, flip, me, layer, early, late, row_share, last_bit):
    tile_count = counts.shape[0]
    scalar = pl.BlockSpec(memory_space=pltpu.SMEM)
    vmem = pl.BlockSpec(memory_space=pltpu.VMEM)
    rows, width = BY * BLOCK, BX * BLOCK
    half = (4, rows // 2, width)
    return pl.pallas_call(
        functools.partial(gather_kernel, tile_count, row_share, last_bit),
        in_specs=[scalar] * 5 + [vmem] * (1 + len(late)),
        out_specs=[vmem] * 3,
        out_shape=[
            jax.ShapeDtypeStruct(half, jnp.float32),
            jax.ShapeDtypeStruct(half, jnp.int16),
            jax.ShapeDtypeStruct((8, LANES), jnp.float32),
        ],
        scratch_shapes=[
            pltpu.VMEM(early.shape, jnp.float32),
            pltpu.VMEM((4, rows, width), jnp.float32),
        ],
        compiler_params=pltpu.CompilerParams(vmem_limit_bytes=GRANT),
        name="gather",
    )(counts, order, flip, me, layer, early, *late)


def blend_kernel(bit, row_share, *refs):
    flip_ref, me_ref, layer_ref, kept_ref, other_ref, kept_out, given_out, image_ref = refs
    front = (layer_ref[0] >> bit & 1) == flip_ref[me_ref[0]]
    kept_open = 1.0 - kept_ref[3]
    other_open = 1.0 - decode(other_ref[3])
    kept_part = jnp.where(front, 1.0, other_open)
    other_part = jnp.where(front, kept_open, 1.0)
    for c in range(4):
        image_ref[c] = kept_part * kept_ref[c] + other_part * decode(other_ref[c])
    split_rows(image_ref, kept_out, given_out, layer_ref[0] >> (bit + 1) & 1, row_share)


def blend(flip, me, layer, kept, other, bit, row_share):
    scalar = pl.BlockSpec(memory_space=pltpu.SMEM)
    vmem = pl.BlockSpec(memory_space=pltpu.VMEM)
    half = (4, kept.shape[1] // 2, kept.shape[2])
    return pl.pallas_call(
        functools.partial(blend_kernel, bit, row_share),
        in_specs=[scalar] * 3 + [vmem] * 2,
        out_specs=[vmem] * 2,
        out_shape=[
            jax.ShapeDtypeStruct(half, jnp.float32),
            jax.ShapeDtypeStruct(half, jnp.int16),
        ],
        scratch_shapes=[pltpu.VMEM(kept.shape, jnp.float32)],
        compiler_params=pltpu.CompilerParams(vmem_limit_bytes=GRANT),
        name="blend",
    )(flip, me, layer, kept, other)


def last_blend(front, kept, coded):
    other = decode(coded)
    front = front[:1][None] > 0.5
    kept_part = jnp.where(front, 1.0, 1.0 - other[3:])
    other_part = jnp.where(front, 1.0 - kept[3:], 1.0)
    return kept_part * kept + other_part * other


def swapped(block, axis, bit):
    count = lax.axis_size(axis)
    return lax.ppermute(block, axis, [(i, i ^ 1 << bit) for i in range(count)])


def body(owned_blocks, slot_counts, brick_order, view_flip, tf_centers, tf_amps):
    tile_count = lax.axis_size("tile")
    depth_count = lax.axis_size("depth")
    step_size = 1.5 / (depth_count * DB * BLOCK)
    me = lax.axis_index("tile").astype(jnp.int32).reshape(1)
    layer = lax.axis_index("depth").astype(jnp.int32).reshape(1)
    counts, order = slot_counts[0], brick_order[0]
    inputs = (counts, order, view_flip, me, tf_centers, tf_amps, owned_blocks[0])
    sent = march(*inputs, step_size)
    arrived = [sent[0]]
    for r in range(1, tile_count):
        route = [(i, (i + r) % tile_count) for i in range(tile_count)]
        arrived.append(lax.ppermute(sent[r], "tile", route))
    early = place_early(counts, order, me, arrived[:tile_count // 2])
    row_share = BY * BLOCK // depth_count
    levels = depth_count.bit_length() - 1
    kept, given, front = gather(
        counts, order, view_flip, me, layer, early, arrived[tile_count // 2:], row_share, levels - 1
    )
    for bit in range(levels - 1):
        other = swapped(given, "depth", bit)
        kept, given = blend(view_flip, me, layer, kept, other, bit, row_share)
    return last_blend(front, kept, swapped(given, "depth", levels - 1))


def solution(mesh):
    in_specs = (P("depth", "tile", None), P("depth", None), P("depth", None), P(), P(), P())
    out_specs = P(None, "depth", "tile")
    return jax.shard_map(body, mesh=mesh, in_specs=in_specs, out_specs=out_specs, check_vma=False)
```

profile of v0, /device:TPU:0, one launch (start us, length us, event | category | flops | bytes accessed | tf_op | source)
XLA Modules:
  0.0 51.1 jit_solution(8670864548848394428)
XLA Ops:
  0.0 0.0 copy-start
  0.0 0.0 copy-start.2
  0.0 0.0 copy-start.1
  0.0 11.2 %march.1 = (s16[8,4,8,128]{3,2,1,0:T(8,128)(2,1)S(1)}, s16[8,4,8,128]{3,2,1,0:T(8,128)(2,1)S(1)}, s16[8,4,8,128]{3,2,1,0:T(8,128)(2,1)S(1)}, s16[8,4,8,128]{3,2,...) custom-call(s32[8]{0:T(128)} %bitcast.12, ...), custom_call_target="tpu_custom_call" | custom-call | tf_op jit(solution)/shard_map/march/pallas_call | solution.py:177
  11.2 16.3 %collective-permute-start = (s16[8,4,8,128]{3,2,1,0:T(8,128)(2,1)S(1)}, s16[8,4,8,128]{3,2,1,0:T(8,128)(2,1)S(1)}, u32[]{:S(2)}, u32[]{:S(2)}) collective-permute-start(s16[8,4,8,128]{3,2,1,0:T(8,128)(2,1)S(1)} %get-tuple-element.19), channel_id=1, source_target_pairs={{0,4},{4,8},{8,12},{12,16},{16,20},{20,24},{24,28},{28,0},{1,5},{5... | collective-permute-start | bytes 196616 | tf_op jit(solution)/shard_map/ppermute | solution.py:369
  27.5 3.4 %collective-permute-start.1 = (s16[8,4,8,128]{3,2,1,0:T(8,128)(2,1)S(1)}, s16[8,4,8,128]{3,2,1,0:T(8,128)(2,1)S(1)}, u32[]{:S(2)}, u32[]{:S(2)}) collective-permute-start(s16[8,4,8,128]{3,2,1,0:T(8,128)(2,1)S(1)} %get-tuple-element.20), channel_id=1, source_target_pairs={{0,8},{4,12},{8,16},{12,20},{16,24},{20,28},{24,0},{28,4},{1,9},{5... | collective-permute-start | bytes 196616 | tf_op jit(solution)/shard_map/ppermute | solution.py:369
  30.8 0.0 collective-permute-start.2
  30.8 5.2 %collective-permute-start.3 = (s16[8,4,8,128]{3,2,1,0:T(8,128)(2,1)S(1)}, s16[8,4,8,128]{3,2,1,0:T(8,128)(2,1)S(1)}, u32[]{:S(2)}, u32[]{:S(2)}) collective-permute-start(s16[8,4,8,128]{3,2,1,0:T(8,128)(2,1)S(1)} %get-tuple-element.22), channel_id=1, source_target_pairs={{0,16},{4,20},{8,24},{12,28},{16,0},{20,4},{24,8},{28,12},{1,17},{... | collective-permute-start | bytes 196616 | tf_op jit(solution)/shard_map/ppermute | solution.py:369
  36.1 0.0 collective-permute-start.4
  36.1 0.0 collective-permute-done.refs_4_
  36.1 2.4 %collective-permute-start.5 = (s16[8,4,8,128]{3,2,1,0:T(8,128)(2,1)S(1)}, s16[8,4,8,128]{3,2,1,0:T(8,128)(2,1)S(1)}, u32[]{:S(2)}, u32[]{:S(2)}) collective-permute-start(s16[8,4,8,128]{3,2,1,0:T(8,128)(2,1)S(1)} %get-tuple-element.24), channel_id=1, source_target_pairs={{0,24},{4,28},{8,0},{12,4},{16,8},{20,12},{24,16},{28,20},{1,25},{... | collective-permute-start | bytes 196616 | tf_op jit(solution)/shard_map/ppermute | solution.py:369
  38.4 0.0 collective-permute-done.1.refs_5_
  38.4 1.5 %collective-permute-start.6 = (s16[8,4,8,128]{3,2,1,0:T(8,128)(2,1)S(1)}, s16[8,4,8,128]{3,2,1,0:T(8,128)(2,1)S(1)}, u32[]{:S(2)}, u32[]{:S(2)}) collective-permute-start(s16[8,4,8,128]{3,2,1,0:T(8,128)(2,1)S(1)} %get-tuple-element.25), channel_id=1, source_target_pairs={{0,28},{4,0},{8,4},{12,8},{16,12},{20,16},{24,20},{28,24},{1,29},{... | collective-permute-start | bytes 196616 | tf_op jit(solution)/shard_map/ppermute | solution.py:369
  39.9 0.0 collective-permute-done.2.refs_6_
  39.9 0.0 copy-done.2
  39.9 0.0 copy-done.1
  39.9 0.7 %place.1.refs_5_ = f32[32,4,8,128]{3,2,1,0:T(8,128)S(1)} custom-call(s32[8]{0:T(128)S(1)} %bitcast.13, s32[8]{0:T(128)S(1)} %bitcast.16, s32[1]{0:T(128)} %bitcast.2.refs_3_.refs_2_.refs_1_, s16[8,4,8,128]{3,2,1,0:T(8,128)(2,1)S(1)} %get-tuple-element.18.refs_3_, s16[8,4,8,128]{3,2,1,0:T(8,128)(2,1)S(1)} %collective-permute-done.refs_4_, ...), custom_call_target="tpu_custom_call" | custom-call | flops 1048576 | bytes 1048576 | tf_op jit(solution)/shard_map/place/pallas_call | solution.py:239
  40.7 0.5 collective-permute-done.3.refs_6_
  41.1 1.0 %collective-permute-done.4.refs_7_ = s16[8,4,8,128]{3,2,1,0:T(8,128)(2,1)S(1)} collective-permute-done((s16[8,4,8,128]{3,2,1,0:T(8,128)(2,1)S(1)}, s16[8,4,8,128]{3,2,1,0:T(8,128)(2,1)S(1)}, u32[]{:S(2)}, u32[]{:S(2)}) %collective-permute-start.4) | collective-permute-done | bytes 65568 | tf_op jit(solution)/shard_map/ppermute | solution.py:369
  42.1 0.4 collective-permute-done.5.refs_8_
  42.5 0.3 collective-permute-done.6.refs_9_
  42.8 0.0 copy-done
  42.8 1.2 %gather.1 = (f32[4,64,128]{2,1,0:T(8,128)S(1)}, s16[4,64,128]{2,1,0:T(8,128)(2,1)S(1)}, f32[8,128]{1,0:T(8,128)S(1)}) custom-call(s32[8]{0:T(128)S(1)} %bitcast.14, s32[8]{0:T(128)S(1)} %bitcast.17, s32[8]{0:T(128)S(1)} %copy-done, s32[1]{0:T(128)} %bitcast.2.refs_3_.refs_2_.refs_1_, s32[1]{0:T(128)} %bitcast.3.refs_4_.refs_2_, ...), custom_call_target="tpu_custom_call" | custom-call | tf_op jit(solution)/shard_map/gather/pallas_call | solution.py:296
  44.0 0.1 collective-permute-start.7
  44.1 1.2 %collective-permute-done.7.refs_4_ = s16[4,64,128]{2,1,0:T(8,128)(2,1)S(1)} collective-permute-done((s16[4,64,128]{2,1,0:T(8,128)(2,1)S(1)}, s16[4,64,128]{2,1,0:T(8,128)(2,1)S(1)}, u32[]{:S(2)}, u32[]{:S(2)}) %collective-permute-start.7) | collective-permute-done | bytes 65568 | tf_op jit(solution)/shard_map/ppermute | solution.py:354
  45.3 0.6 %blend.1 = (f32[4,32,128]{2,1,0:T(8,128)S(1)}, s16[4,32,128]{2,1,0:T(8,128)(2,1)S(1)}) custom-call(s32[8]{0:T(128)S(1)} %copy-done, s32[1]{0:T(128)} %bitcast.2.refs_3_.refs_2_.refs_1_, s32[1]{0:T(128)} %bitcast.3.refs_4_.refs_2_, f32[4,64,128]{2,1,0:T(8,128)S(1)} %get-tuple-element.27.refs_3_, s16[4,64,128]{2,1,0:T(8,128)(2,1)S(1)} %collective-permute-done.7.refs_4_), custom_call_target="tpu_custom_call" | custom-call | tf_op jit(solution)/shard_map/blend/pallas_call | solution.py:330
  46.0 2.6 %collective-permute-start.8 = (s16[4,32,128]{2,1,0:T(8,128)(2,1)S(1)}, s16[4,32,128]{2,1,0:T(8,128)(2,1)S(1)}, u32[]{:S(2)}, u32[]{:S(2)}) collective-permute-start(s16[4,32,128]{2,1,0:T(8,128)(2,1)S(1)} %get-tuple-element.29), channel_id=1, source_target_pairs={{0,2},{1,3},{2,0},{3,1},{4,6},{5,7},{6,4},{7,5},{8,10},{9,11},{10,... | collective-permute-start | bytes 98312 | tf_op jit(solution)/shard_map/ppermute | solution.py:354
  48.6 1.9 %collective-permute-done.8 = s16[4,32,128]{2,1,0:T(8,128)(2,1)S(1)} collective-permute-done((s16[4,32,128]{2,1,0:T(8,128)(2,1)S(1)}, s16[4,32,128]{2,1,0:T(8,128)(2,1)S(1)}, u32[]{:S(2)}, u32[]{:S(2)}) %collective-permute-start.8) | collective-permute-done | bytes 32800 | tf_op jit(solution)/shard_map/ppermute | solution.py:354
  50.5 0.7 %multiply_add_fusion = f32[4,32,128]{2,1,0:T(8,128)} fusion(f32[4,32,128]{2,1,0:T(8,128)S(1)} %get-tuple-element.30, f32[32,128]{1,0:T(8,128)S(1)} %get-tuple-element.32, f32[32,128]{1,0:T(8,128)S(1)} %get-tuple-element.31, s16[4,32,128]{2,1,0:T(8,128)(2,1)S(1)} %collective-permute-done.8), kind=kLoop, calls=%fused_computation | loop fusion | flops 147456 | bytes 196608 | tf_op jit(solution)/shard_map/add | solution.py:349
  (3 shorter events, 0.0 us)
Async XLA Ops:
  0.0 42.8 %copy-start = (s32[8]{0:T(128)S(1)}, s32[8]{0:T(128)}, u32[]{:S(2)}) copy-start(s32[8]{0:T(128)} %refs_0_.1) | copy-start | bytes 100
  0.0 39.9 %copy-start.2 = (s32[1,8]{1,0:T(1,128)S(1)}, s32[1,8]{1,0:T(1,128)}, u32[]{:S(2)}) copy-start(s32[1,8]{1,0:T(1,128)} %param.8) | copy-start | bytes 100
  0.0 39.9 %copy-start.1 = (s32[1,8]{1,0:T(1,128)S(1)}, s32[1,8]{1,0:T(1,128)}, u32[]{:S(2)}) copy-start(s32[1,8]{1,0:T(1,128)} %param.7) | copy-start | bytes 100
  11.2 24.9 %collective-permute-start = (s16[8,4,8,128]{3,2,1,0:T(8,128)(2,1)S(1)}, s16[8,4,8,128]{3,2,1,0:T(8,128)(2,1)S(1)}, u32[]{:S(2)}, u32[]{:S(2)}) collective-permute-start(s16[8,4,8,128]{3,2,1,0:T(8,128)(2,1)S(1)} %get-tuple-element.19), channel_id=1, source_target_pairs={{0,4},{4,8},{8,12},{12,16},{16,20},{20,24},{24,28},{28,0},{1,5},{5... | collective-permute-start | bytes 196616 | tf_op jit(solution)/shard_map/ppermute | solution.py:369
  27.5 11.0 %collective-permute-start.1 = (s16[8,4,8,128]{3,2,1,0:T(8,128)(2,1)S(1)}, s16[8,4,8,128]{3,2,1,0:T(8,128)(2,1)S(1)}, u32[]{:S(2)}, u32[]{:S(2)}) collective-permute-start(s16[8,4,8,128]{3,2,1,0:T(8,128)(2,1)S(1)} %get-tuple-element.20), channel_id=1, source_target_pairs={{0,8},{4,12},{8,16},{12,20},{16,24},{20,28},{24,0},{28,4},{1,9},{5... | collective-permute-start | bytes 196616 | tf_op jit(solution)/shard_map/ppermute | solution.py:369
  30.8 9.1 %collective-permute-start.2 = (s16[8,4,8,128]{3,2,1,0:T(8,128)(2,1)S(1)}, s16[8,4,8,128]{3,2,1,0:T(8,128)(2,1)S(1)}, u32[]{:S(2)}, u32[]{:S(2)}) collective-permute-start(s16[8,4,8,128]{3,2,1,0:T(8,128)(2,1)S(1)} %get-tuple-element.21), channel_id=1, source_target_pairs={{0,12},{4,16},{8,20},{12,24},{16,28},{20,0},{24,4},{28,8},{1,13},{... | collective-permute-start | bytes 196616 | tf_op jit(solution)/shard_map/ppermute | solution.py:369
  30.8 10.3 %collective-permute-start.3 = (s16[8,4,8,128]{3,2,1,0:T(8,128)(2,1)S(1)}, s16[8,4,8,128]{3,2,1,0:T(8,128)(2,1)S(1)}, u32[]{:S(2)}, u32[]{:S(2)}) collective-permute-start(s16[8,4,8,128]{3,2,1,0:T(8,128)(2,1)S(1)} %get-tuple-element.22), channel_id=1, source_target_pairs={{0,16},{4,20},{8,24},{12,28},{16,0},{20,4},{24,8},{28,12},{1,17},{... | collective-permute-start | bytes 196616 | tf_op jit(solution)/shard_map/ppermute | solution.py:369
  36.1 6.1 %collective-permute-start.4 = (s16[8,4,8,128]{3,2,1,0:T(8,128)(2,1)S(1)}, s16[8,4,8,128]{3,2,1,0:T(8,128)(2,1)S(1)}, u32[]{:S(2)}, u32[]{:S(2)}) collective-permute-start(s16[8,4,8,128]{3,2,1,0:T(8,128)(2,1)S(1)} %get-tuple-element.23), channel_id=1, source_target_pairs={{0,20},{4,24},{8,28},{12,0},{16,4},{20,8},{24,12},{28,16},{1,21},{... | collective-permute-start | bytes 196616 | tf_op jit(solution)/shard_map/ppermute | solution.py:369
  36.1 6.4 %collective-permute-start.5 = (s16[8,4,8,128]{3,2,1,0:T(8,128)(2,1)S(1)}, s16[8,4,8,128]{3,2,1,0:T(8,128)(2,1)S(1)}, u32[]{:S(2)}, u32[]{:S(2)}) collective-permute-start(s16[8,4,8,128]{3,2,1,0:T(8,128)(2,1)S(1)} %get-tuple-element.24), channel_id=1, source_target_pairs={{0,24},{4,28},{8,0},{12,4},{16,8},{20,12},{24,16},{28,20},{1,25},{... | collective-permute-start | bytes 196616 | tf_op jit(solution)/shard_map/ppermute | solution.py:369
  38.4 4.4 %collective-permute-start.6 = (s16[8,4,8,128]{3,2,1,0:T(8,128)(2,1)S(1)}, s16[8,4,8,128]{3,2,1,0:T(8,128)(2,1)S(1)}, u32[]{:S(2)}, u32[]{:S(2)}) collective-permute-start(s16[8,4,8,128]{3,2,1,0:T(8,128)(2,1)S(1)} %get-tuple-element.25), channel_id=1, source_target_pairs={{0,28},{4,0},{8,4},{12,8},{16,12},{20,16},{24,20},{28,24},{1,29},{... | collective-permute-start | bytes 196616 | tf_op jit(solution)/shard_map/ppermute | solution.py:369
  44.0 1.3 %collective-permute-start.7 = (s16[4,64,128]{2,1,0:T(8,128)(2,1)S(1)}, s16[4,64,128]{2,1,0:T(8,128)(2,1)S(1)}, u32[]{:S(2)}, u32[]{:S(2)}) collective-permute-start(s16[4,64,128]{2,1,0:T(8,128)(2,1)S(1)} %get-tuple-element.28), channel_id=1, source_target_pairs={{0,1},{1,0},{2,3},{3,2},{4,5},{5,4},{6,7},{7,6},{8,9},{9,8},{10,11... | collective-permute-start | bytes 196616 | tf_op jit(solution)/shard_map/ppermute | solution.py:354
  46.0 4.5 %collective-permute-start.8 = (s16[4,32,128]{2,1,0:T(8,128)(2,1)S(1)}, s16[4,32,128]{2,1,0:T(8,128)(2,1)S(1)}, u32[]{:S(2)}, u32[]{:S(2)}) collective-permute-start(s16[4,32,128]{2,1,0:T(8,128)(2,1)S(1)} %get-tuple-element.29), channel_id=1, source_target_pairs={{0,2},{1,3},{2,0},{3,1},{4,6},{5,7},{6,4},{7,5},{8,10},{9,11},{10,... | collective-permute-start | bytes 98312 | tf_op jit(solution)/shard_map/ppermute | solution.py:354
where the time goes:
time: 52 us; the launch traced here: 51.1 us
  starting transfers between devices  31.4 us (60%)
  Pallas kernels  13.7 us (26%)
  waiting for transfers between devices  5.31 us (10%)
  other arithmetic  0.7 us (1%)
    ppermute x7, starting transfers between devices, body(): arrived.append(lax.ppermute(sent[r], 'tile', route))  28.7 us
    pallas_call x1, Pallas kernels, march(): pl.pallas_call(functools.partial(march_kernel, step_size, tile_count, til...  11.2 us
    ppermute x2, waiting for transfers between devices, swapped(): return lax.ppermute(block, axis, [(i, i ^ 1 << bit) for i in range(count)])  3.13 us
    ppermute x2, starting transfers between devices, swapped(): return lax.ppermute(block, axis, [(i, i ^ 1 << bit) for i in range(count)])  2.65 us
    ppermute x7, waiting for transfers between devices, body(): arrived.append(lax.ppermute(sent[r], 'tile', route))  2.18 us
    pallas_call x1, Pallas kernels, gather(): pl.pallas_call(functools.partial(gather_kernel, tile_count, row_share, la...  1.17 us
  transfers between devices with their start and end apart: 9, of which 6 were waited for; matrix products, arithmetic and copies ran while one was open for 0% of the time, Pallas kernels for 1%

commit v1 on v0

--- a/solution.py
+++ b/solution.py
@@ -20,7 +20,7 @@
 LOG2E = math.log2(math.e)
 ROOT = math.sqrt(BUMP_SCALE * LOG2E)
 CODE_TOP = 65535.0
-CODE_MID = 32767.5
+CODE_MID = 32768.0
 GRANT = 12 << 20
 SPAN = 512
 GROUPS = PIXELS // SPAN

time: 52 us -> 52.2 us (level); the launches traced: 51.1 us -> 52.1 us
  starting transfers between devices: 31.4 us -> 23.5 us
  Pallas kernels: 13.7 us -> 19.2 us
  waiting for transfers between devices: 5.31 us -> 8.54 us
    pallas_call x1, Pallas kernels: 11.2 us -> 16.6 us  [march(): pl.pallas_call(functools.partial(march_kernel, step_size, tile_count, til...]
    ppermute x7, starting transfers between devices: 28.7 us -> 23.4 us  [body(): arrived.append(lax.ppermute(sent[r], 'tile', route))]
    ppermute x2, starting transfers between devices: 2.65 us -> 0.14 us  [swapped(): return lax.ppermute(block, axis, [(i, i ^ 1 << bit) for i in range(count)])]
    ppermute x2, waiting for transfers between devices: 3.13 us -> 5.13 us  [swapped(): return lax.ppermute(block, axis, [(i, i ^ 1 << bit) for i in range(count)])]
    ppermute x7, waiting for transfers between devices: 2.18 us -> 3.41 us  [body(): arrived.append(lax.ppermute(sent[r], 'tile', route))]
  transfers between devices with their start and end apart: 9 -> 9, of which waited for: 6 -> 4; matrix products, arithmetic and copies ran while one was open for 0% -> 0% of each run, Pallas kernels for 1% -> 2%
where the time goes in v1:
time: 52.2 us; the launch traced here: 52.1 us
  starting transfers between devices  23.5 us (45%)
  Pallas kernels  19.2 us (37%)
  waiting for transfers between devices  8.54 us (16%)
  other arithmetic  0.7 us (1%)
    ppermute x7, starting transfers between devices, body(): arrived.append(lax.ppermute(sent[r], 'tile', route))  23.4 us
    pallas_call x1, Pallas kernels, march(): pl.pallas_call(functools.partial(march_kernel, step_size, tile_count, til...  16.6 us
    ppermute x2, waiting for transfers between devices, swapped(): return lax.ppermute(block, axis, [(i, i ^ 1 << bit) for i in range(count)])  5.13 us
    ppermute x7, waiting for transfers between devices, body(): arrived.append(lax.ppermute(sent[r], 'tile', route))  3.41 us
    pallas_call x1, Pallas kernels, gather(): pl.pallas_call(functools.partial(gather_kernel, tile_count, row_share, la...  1.09 us
  transfers between devices with their start and end apart: 9, of which 4 were waited for; matrix products, arithmetic and copies ran while one was open for 0% of the time, Pallas kernels for 2%

profile of v1, /device:TPU:0, one launch (start us, length us, event | category | flops | bytes accessed | tf_op | source)
XLA Modules:
  0.0 52.1 jit_solution(10490814471655610178)
XLA Ops:
  0.0 0.0 copy-start
  0.0 0.0 copy-start.2
  0.0 0.0 copy-start.1
  0.0 16.6 %march.1 = (s16[8,4,8,128]{3,2,1,0:T(8,128)(2,1)S(1)}, s16[8,4,8,128]{3,2,1,0:T(8,128)(2,1)S(1)}, s16[8,4,8,128]{3,2,1,0:T(8,128)(2,1)S(1)}, s16[8,4,8,128]{3,2,...) custom-call(s32[8]{0:T(128)} %bitcast.12, ...), custom_call_target="tpu_custom_call" | custom-call | tf_op jit(solution)/shard_map/march/pallas_call | solution.py:177
  16.7 0.1 collective-permute-start
  16.7 10.1 %collective-permute-start.1 = (s16[8,4,8,128]{3,2,1,0:T(8,128)(2,1)S(1)}, s16[8,4,8,128]{3,2,1,0:T(8,128)(2,1)S(1)}, u32[]{:S(2)}, u32[]{:S(2)}) collective-permute-start(s16[8,4,8,128]{3,2,1,0:T(8,128)(2,1)S(1)} %get-tuple-element.20), channel_id=1, source_target_pairs={{0,8},{4,12},{8,16},{12,20},{16,24},{20,28},{24,0},{28,4},{1,9},{5... | collective-permute-start | bytes 196616 | tf_op jit(solution)/shard_map/ppermute | solution.py:369
  26.8 6.6 %collective-permute-start.2 = (s16[8,4,8,128]{3,2,1,0:T(8,128)(2,1)S(1)}, s16[8,4,8,128]{3,2,1,0:T(8,128)(2,1)S(1)}, u32[]{:S(2)}, u32[]{:S(2)}) collective-permute-start(s16[8,4,8,128]{3,2,1,0:T(8,128)(2,1)S(1)} %get-tuple-element.21), channel_id=1, source_target_pairs={{0,12},{4,16},{8,20},{12,24},{16,28},{20,0},{24,4},{28,8},{1,13},{... | collective-permute-start | bytes 196616 | tf_op jit(solution)/shard_map/ppermute | solution.py:369
  33.4 0.0 collective-permute-start.3
  33.4 3.8 %collective-permute-start.4 = (s16[8,4,8,128]{3,2,1,0:T(8,128)(2,1)S(1)}, s16[8,4,8,128]{3,2,1,0:T(8,128)(2,1)S(1)}, u32[]{:S(2)}, u32[]{:S(2)}) collective-permute-start(s16[8,4,8,128]{3,2,1,0:T(8,128)(2,1)S(1)} %get-tuple-element.23), channel_id=1, source_target_pairs={{0,20},{4,24},{8,28},{12,0},{16,4},{20,8},{24,12},{28,16},{1,21},{... | collective-permute-start | bytes 196616 | tf_op jit(solution)/shard_map/ppermute | solution.py:369
  37.1 0.0 collective-permute-done.refs_4_
  37.1 2.9 %collective-permute-start.5 = (s16[8,4,8,128]{3,2,1,0:T(8,128)(2,1)S(1)}, s16[8,4,8,128]{3,2,1,0:T(8,128)(2,1)S(1)}, u32[]{:S(2)}, u32[]{:S(2)}) collective-permute-start(s16[8,4,8,128]{3,2,1,0:T(8,128)(2,1)S(1)} %get-tuple-element.24), channel_id=1, source_target_pairs={{0,24},{4,28},{8,0},{12,4},{16,8},{20,12},{24,16},{28,20},{1,25},{... | collective-permute-start | bytes 196616 | tf_op jit(solution)/shard_map/ppermute | solution.py:369
  40.1 0.0 collective-permute-done.1.refs_5_
  40.1 0.0 collective-permute-start.6
  40.1 0.0 collective-permute-done.2.refs_6_
  40.1 0.0 copy-done.2
  40.1 0.0 copy-done.1
  40.1 0.8 %place.1.refs_5_ = f32[32,4,8,128]{3,2,1,0:T(8,128)S(1)} custom-call(s32[8]{0:T(128)S(1)} %bitcast.13, s32[8]{0:T(128)S(1)} %bitcast.16, s32[1]{0:T(128)} %bitcast.2.refs_3_.refs_2_.refs_1_, s16[8,4,8,128]{3,2,1,0:T(8,128)(2,1)S(1)} %get-tuple-element.18.refs_3_, s16[8,4,8,128]{3,2,1,0:T(8,128)(2,1)S(1)} %collective-permute-done.refs_4_, ...), custom_call_target="tpu_custom_call" | custom-call | flops 1048576 | bytes 1048576 | tf_op jit(solution)/shard_map/place/pallas_call | solution.py:239
  40.9 0.0 collective-permute-done.3.refs_6_
  40.9 0.0 collective-permute-done.4.refs_7_
  40.9 1.0 %collective-permute-done.5.refs_8_ = s16[8,4,8,128]{3,2,1,0:T(8,128)(2,1)S(1)} collective-permute-done((s16[8,4,8,128]{3,2,1,0:T(8,128)(2,1)S(1)}, s16[8,4,8,128]{3,2,1,0:T(8,128)(2,1)S(1)}, u32[]{:S(2)}, u32[]{:S(2)}) %collective-permute-start.5) | collective-permute-done | bytes 65568 | tf_op jit(solution)/shard_map/ppermute | solution.py:369
  42.0 2.4 %collective-permute-done.6.refs_9_ = s16[8,4,8,128]{3,2,1,0:T(8,128)(2,1)S(1)} collective-permute-done((s16[8,4,8,128]{3,2,1,0:T(8,128)(2,1)S(1)}, s16[8,4,8,128]{3,2,1,0:T(8,128)(2,1)S(1)}, u32[]{:S(2)}, u32[]{:S(2)}) %collective-permute-start.6) | collective-permute-done | bytes 65568 | tf_op jit(solution)/shard_map/ppermute | solution.py:369
  44.3 0.0 copy-done
  44.3 1.1 %gather.1 = (f32[4,64,128]{2,1,0:T(8,128)S(1)}, s16[4,64,128]{2,1,0:T(8,128)(2,1)S(1)}, f32[8,128]{1,0:T(8,128)S(1)}) custom-call(s32[8]{0:T(128)S(1)} %bitcast.14, s32[8]{0:T(128)S(1)} %bitcast.17, s32[8]{0:T(128)S(1)} %copy-done, s32[1]{0:T(128)} %bitcast.2.refs_3_.refs_2_.refs_1_, s32[1]{0:T(128)} %bitcast.3.refs_4_.refs_2_, ...), custom_call_target="tpu_custom_call" | custom-call | tf_op jit(solution)/shard_map/gather/pallas_call | solution.py:296
  45.4 0.1 collective-permute-start.7
  45.5 1.2 %collective-permute-done.7.refs_4_ = s16[4,64,128]{2,1,0:T(8,128)(2,1)S(1)} collective-permute-done((s16[4,64,128]{2,1,0:T(8,128)(2,1)S(1)}, s16[4,64,128]{2,1,0:T(8,128)(2,1)S(1)}, u32[]{:S(2)}, u32[]{:S(2)}) %collective-permute-start.7) | collective-permute-done | bytes 65568 | tf_op jit(solution)/shard_map/ppermute | solution.py:354
  46.8 0.6 %blend.1 = (f32[4,32,128]{2,1,0:T(8,128)S(1)}, s16[4,32,128]{2,1,0:T(8,128)(2,1)S(1)}) custom-call(s32[8]{0:T(128)S(1)} %copy-done, s32[1]{0:T(128)} %bitcast.2.refs_3_.refs_2_.refs_1_, s32[1]{0:T(128)} %bitcast.3.refs_4_.refs_2_, f32[4,64,128]{2,1,0:T(8,128)S(1)} %get-tuple-element.27.refs_3_, s16[4,64,128]{2,1,0:T(8,128)(2,1)S(1)} %collective-permute-done.7.refs_4_), custom_call_target="tpu_custom_call" | custom-call | tf_op jit(solution)/shard_map/blend/pallas_call | solution.py:330
  47.4 0.1 collective-permute-start.8
  47.5 3.9 %collective-permute-done.8 = s16[4,32,128]{2,1,0:T(8,128)(2,1)S(1)} collective-permute-done((s16[4,32,128]{2,1,0:T(8,128)(2,1)S(1)}, s16[4,32,128]{2,1,0:T(8,128)(2,1)S(1)}, u32[]{:S(2)}, u32[]{:S(2)}) %collective-permute-start.8) | collective-permute-done | bytes 32800 | tf_op jit(solution)/shard_map/ppermute | solution.py:354
  51.4 0.7 %multiply_add_fusion = f32[4,32,128]{2,1,0:T(8,128)} fusion(f32[4,32,128]{2,1,0:T(8,128)S(1)} %get-tuple-element.30, f32[32,128]{1,0:T(8,128)S(1)} %get-tuple-element.32, f32[32,128]{1,0:T(8,128)S(1)} %get-tuple-element.31, s16[4,32,128]{2,1,0:T(8,128)(2,1)S(1)} %collective-permute-done.8), kind=kLoop, calls=%fused_computation | loop fusion | flops 147456 | bytes 196608 | tf_op jit(solution)/shard_map/add | solution.py:349
  (3 shorter events, 0.0 us)
Async XLA Ops:
  0.0 44.3 %copy-start = (s32[8]{0:T(128)S(1)}, s32[8]{0:T(128)}, u32[]{:S(2)}) copy-start(s32[8]{0:T(128)} %refs_0_.1) | copy-start | bytes 100
  0.0 40.1 %copy-start.2 = (s32[1,8]{1,0:T(1,128)S(1)}, s32[1,8]{1,0:T(1,128)}, u32[]{:S(2)}) copy-start(s32[1,8]{1,0:T(1,128)} %param.8) | copy-start | bytes 100
  0.0 40.1 %copy-start.1 = (s32[1,8]{1,0:T(1,128)S(1)}, s32[1,8]{1,0:T(1,128)}, u32[]{:S(2)}) copy-start(s32[1,8]{1,0:T(1,128)} %param.7) | copy-start | bytes 100
  16.7 20.5 %collective-permute-start = (s16[8,4,8,128]{3,2,1,0:T(8,128)(2,1)S(1)}, s16[8,4,8,128]{3,2,1,0:T(8,128)(2,1)S(1)}, u32[]{:S(2)}, u32[]{:S(2)}) collective-permute-start(s16[8,4,8,128]{3,2,1,0:T(8,128)(2,1)S(1)} %get-tuple-element.19), channel_id=1, source_target_pairs={{0,4},{4,8},{8,12},{12,16},{16,20},{20,24},{24,28},{28,0},{1,5},{5... | collective-permute-start | bytes 196616 | tf_op jit(solution)/shard_map/ppermute | solution.py:369
  16.7 23.3 %collective-permute-start.1 = (s16[8,4,8,128]{3,2,1,0:T(8,128)(2,1)S(1)}, s16[8,4,8,128]{3,2,1,0:T(8,128)(2,1)S(1)}, u32[]{:S(2)}, u32[]{:S(2)}) collective-permute-start(s16[8,4,8,128]{3,2,1,0:T(8,128)(2,1)S(1)} %get-tuple-element.20), channel_id=1, source_target_pairs={{0,8},{4,12},{8,16},{12,20},{16,24},{20,28},{24,0},{28,4},{1,9},{5... | collective-permute-start | bytes 196616 | tf_op jit(solution)/shard_map/ppermute | solution.py:369
  26.8 13.3 %collective-permute-start.2 = (s16[8,4,8,128]{3,2,1,0:T(8,128)(2,1)S(1)}, s16[8,4,8,128]{3,2,1,0:T(8,128)(2,1)S(1)}, u32[]{:S(2)}, u32[]{:S(2)}) collective-permute-start(s16[8,4,8,128]{3,2,1,0:T(8,128)(2,1)S(1)} %get-tuple-element.21), channel_id=1, source_target_pairs={{0,12},{4,16},{8,20},{12,24},{16,28},{20,0},{24,4},{28,8},{1,13},{... | collective-permute-start | bytes 196616 | tf_op jit(solution)/shard_map/ppermute | solution.py:369
  33.4 7.5 %collective-permute-start.3 = (s16[8,4,8,128]{3,2,1,0:T(8,128)(2,1)S(1)}, s16[8,4,8,128]{3,2,1,0:T(8,128)(2,1)S(1)}, u32[]{:S(2)}, u32[]{:S(2)}) collective-permute-start(s16[8,4,8,128]{3,2,1,0:T(8,128)(2,1)S(1)} %get-tuple-element.22), channel_id=1, source_target_pairs={{0,16},{4,20},{8,24},{12,28},{16,0},{20,4},{24,8},{28,12},{1,17},{... | collective-permute-start | bytes 196616 | tf_op jit(solution)/shard_map/ppermute | solution.py:369
  33.4 7.5 %collective-permute-start.4 = (s16[8,4,8,128]{3,2,1,0:T(8,128)(2,1)S(1)}, s16[8,4,8,128]{3,2,1,0:T(8,128)(2,1)S(1)}, u32[]{:S(2)}, u32[]{:S(2)}) collective-permute-start(s16[8,4,8,128]{3,2,1,0:T(8,128)(2,1)S(1)} %get-tuple-element.23), channel_id=1, source_target_pairs={{0,20},{4,24},{8,28},{12,0},{16,4},{20,8},{24,12},{28,16},{1,21},{... | collective-permute-start | bytes 196616 | tf_op jit(solution)/shard_map/ppermute | solution.py:369
  37.1 4.8 %collective-permute-start.5 = (s16[8,4,8,128]{3,2,1,0:T(8,128)(2,1)S(1)}, s16[8,4,8,128]{3,2,1,0:T(8,128)(2,1)S(1)}, u32[]{:S(2)}, u32[]{:S(2)}) collective-permute-start(s16[8,4,8,128]{3,2,1,0:T(8,128)(2,1)S(1)} %get-tuple-element.24), channel_id=1, source_target_pairs={{0,24},{4,28},{8,0},{12,4},{16,8},{20,12},{24,16},{28,20},{1,25},{... | collective-permute-start | bytes 196616 | tf_op jit(solution)/shard_map/ppermute | solution.py:369
  40.1 4.3 %collective-permute-start.6 = (s16[8,4,8,128]{3,2,1,0:T(8,128)(2,1)S(1)}, s16[8,4,8,128]{3,2,1,0:T(8,128)(2,1)S(1)}, u32[]{:S(2)}, u32[]{:S(2)}) collective-permute-start(s16[8,4,8,128]{3,2,1,0:T(8,128)(2,1)S(1)} %get-tuple-element.25), channel_id=1, source_target_pairs={{0,28},{4,0},{8,4},{12,8},{16,12},{20,16},{24,20},{28,24},{1,29},{... | collective-permute-start | bytes 196616 | tf_op jit(solution)/shard_map/ppermute | solution.py:369
  45.4 1.3 %collective-permute-start.7 = (s16[4,64,128]{2,1,0:T(8,128)(2,1)S(1)}, s16[4,64,128]{2,1,0:T(8,128)(2,1)S(1)}, u32[]{:S(2)}, u32[]{:S(2)}) collective-permute-start(s16[4,64,128]{2,1,0:T(8,128)(2,1)S(1)} %get-tuple-element.28), channel_id=1, source_target_pairs={{0,1},{1,0},{2,3},{3,2},{4,5},{5,4},{6,7},{7,6},{8,9},{9,8},{10,11... | collective-permute-start | bytes 196616 | tf_op jit(solution)/shard_map/ppermute | solution.py:354
  47.4 4.0 %collective-permute-start.8 = (s16[4,32,128]{2,1,0:T(8,128)(2,1)S(1)}, s16[4,32,128]{2,1,0:T(8,128)(2,1)S(1)}, u32[]{:S(2)}, u32[]{:S(2)}) collective-permute-start(s16[4,32,128]{2,1,0:T(8,128)(2,1)S(1)} %get-tuple-element.29), channel_id=1, source_target_pairs={{0,2},{1,3},{2,0},{3,1},{4,6},{5,7},{6,4},{7,5},{8,10},{9,11},{10,... | collective-permute-start | bytes 98312 | tf_op jit(solution)/shard_map/ppermute | solution.py:354
